TPU v7x, 256 devices: a whole 4x4x8 slice. The times are simulated.
256 devices in a mesh: tok: 64 (over x, z, core), feat: 4 (over y).
Axes of the slice: x: 4, y: 4, z: 8, core: 2. Of those that a mesh axis runs over, the one named last changes fastest.
Arguments:
- queries: bfloat16 [8192, 4096], P('tok', 'feat'), may hold values from -12 to 12
- keys: bfloat16 [8192, 1024], P('tok', 'feat'), may hold values from -12 to 12
- values: bfloat16 [8192, 1024], P('tok', 'feat'), may hold values from -6 to 6
- out_weight: bfloat16 [4096, 4096], P('feat', 'tok'), may hold values from -0.09375 to 0.09375
- doc_lengths: int32 [6], replicated, may hold values from 1 to 5120, 8192 in all
Outputs:
- mixed: bfloat16 [8192, 4096], P('tok', 'feat')
Inputs may be any that keep to these rules, and one draw needn't show every extreme that they name: `doc_lengths`: the lengths sum to 8192, and the largest is exactly 5120.
All inputs are finite; a program needn't handle non-finite values.
Results may differ from a plain program's by a relative error of at most 0.012.
The roundings to bfloat16 on the way count: a program that leaves them out, or rounds other values in their place, can miss the bound.
Values may be sent and summed in bfloat16 or wider, within the bound.
A program may use at most 64 MiB of HBM per device.

v0:
```python
import jax
import jax.numpy as jnp
from jax import lax
from jax.sharding import PartitionSpec as P

HD = 128
ROPE_BASE = 500000.0
NEG_FILL = -1e30


def locate(token_index, doc_lengths):
    doc_ends = jnp.cumsum(doc_lengths)
    starts = doc_ends - doc_lengths
    doc_ids = jnp.sum((token_index[:, None] >= doc_ends[None, :]).astype(jnp.int32), axis=1)
    number = jnp.arange(doc_lengths.shape[0], dtype=jnp.int32)
    first_token = jnp.sum(
        jnp.where(doc_ids[:, None] == number[None, :], starts[None, :], 0), axis=1
    )
    return (doc_ids, token_index - first_token)


def rotary(tensor, positions):
    half_size = tensor.shape[-1] // 2
    frequency = ROPE_BASE ** (-(jnp.arange(half_size, dtype=jnp.float32) * 2.0 / tensor.shape[-1]))
    angles = positions.astype(jnp.float32)[:, None] * frequency[None, :]
    cosine = jnp.cos(angles)[:, None, :]
    sine_part = jnp.sin(angles)[:, None, :]
    first_half = tensor[..., :half_size]
    second_half = tensor[..., half_size:]
    return jnp.concatenate(
        [
            first_half * cosine - second_half * sine_part,
            second_half * cosine + first_half * sine_part,
        ],
        axis=-1,
    )


def pick_block(extent):
    for candidate in (512, 256, 128):
        return candidate
    return extent


def shards(queries, keys, values, out_weight, doc_lengths):
    my_index = lax.axis_index("tok")
    local_rows = queries.shape[0]
    local_heads = queries.shape[1] // HD
    kv_local = keys.shape[1] // HD
    group_size = local_heads // kv_local
    scale_factor = HD ** (-0.5)
    own_index = my_index * local_rows + jnp.arange(local_rows, dtype=jnp.int32)
    own_docs, own_positions = locate(own_index, doc_lengths)
    rotated_q = rotary(
        queries.astype(jnp.float32).reshape(local_rows, local_heads, HD), own_positions
    ).astype(jnp.bfloat16)
    rotated_k = rotary(
        keys.astype(jnp.float32).reshape(local_rows, kv_local, HD), own_positions
    ).astype(jnp.bfloat16)
    rotated_k = rotated_k.reshape(local_rows, kv_local * HD)

    def fresh(query_rows):
        running_max = jnp.full((kv_local, group_size, query_rows), NEG_FILL, jnp.float32)
        totals = jnp.zeros((kv_local, group_size, query_rows), jnp.float32)
        weighted = jnp.zeros((kv_local, group_size, query_rows, HD), jnp.float32)
        return (running_max, totals, weighted)

    def absorb(carry_state, query_block, query_index, key_piece, value_piece, offset):
        query_docs, query_positions = locate(query_index, doc_lengths)
        doc_begin = query_index[0] - query_positions[0]
        last_index = query_index[-1]
        extent = key_piece.shape[0]
        needed = (offset + extent > doc_begin) & (offset <= last_index)
        block_rows = pick_block(extent)

        def sweep_keys(state_in):

            def one_block(block_number, state_now):
                running_max, totals, weighted = state_now
                first_key = block_number * block_rows
                key_tile = lax.dynamic_slice_in_dim(key_piece, first_key, block_rows, 0).reshape(
                    block_rows, kv_local, HD
                )
                value_tile = lax.dynamic_slice_in_dim(
                    value_piece, first_key, block_rows, 0
                ).reshape(block_rows, kv_local, HD)
                key_index = first_key + jnp.arange(block_rows, dtype=jnp.int32)
                key_docs, key_positions = locate(key_index, doc_lengths)
                scores = (
                    jnp.einsum(
                        "qgjd,kgd->gjqk", query_block, key_tile, preferred_element_type=jnp.float32
                    )
                    * scale_factor
                )
                visible = (query_docs[:, None] == key_docs[None, :]) & (
                    key_index[None, :] <= query_index[:, None]
                )
                scores = jnp.where(visible, scores, NEG_FILL)
                new_max = jnp.maximum(running_max, jnp.max(scores, axis=-1))
                factor = jnp.exp(running_max - new_max)
                weights = jnp.where(visible, jnp.exp(scores - new_max[..., None]), 0.0)
                totals = totals * factor + jnp.sum(weights, axis=-1)
                update = jnp.einsum(
                    "gjqk,kgd->gjqd",
                    weights.astype(jnp.bfloat16),
                    value_tile,
                    preferred_element_type=jnp.float32,
                )
                weighted = weighted * factor[..., None] + update
                return (new_max, totals, weighted)

            return lax.fori_loop(0, extent // block_rows, one_block, state_in)

        return lax.cond(needed, sweep_keys, lambda state_in: state_in, carry_state)

    def finish(carry_state):
        running_max, totals, weighted = carry_state
        output = weighted / totals[..., None]
        query_rows = output.shape[2]
        return (
            output.transpose(2, 0, 1, 3).reshape(query_rows, local_heads * HD).astype(jnp.bfloat16)
        )

    groups = [(rotated_q, own_index)]
    query_sets = [
        (member[0].reshape(member[0].shape[0], kv_local, group_size, HD), member[1])
        for member in groups
    ]

    def fold_keys(states, pieces, offset):
        return tuple(
            (
                absorb(state_now, member[0], member[1], pieces[0], pieces[1], offset)
                for state_now, member in zip(states, query_sets)
            )
        )

    initial = tuple((fresh(member[0].shape[0]) for member in query_sets))
    states = fold_keys(
        initial,
        (
            lax.all_gather(rotated_k, "tok", axis=0, tiled=True),
            lax.all_gather(values, "tok", axis=0, tiled=True),
        ),
        jnp.int32(0),
    )
    results = [finish(state_now) for state_now in states]
    attended = results[0]
    partial_terms = jnp.dot(
        attended,
        lax.all_gather(out_weight, "tok", axis=1, tiled=True),
        preferred_element_type=jnp.float32,
    )
    return lax.psum_scatter(
        partial_terms.astype(jnp.bfloat16), "feat", scatter_dimension=1, tiled=True
    )


def solution(mesh):
    in_specs = (P("tok", "feat"), P("tok", "feat"), P("tok", "feat"), P("feat", "tok"), P())
    out_specs = P("tok", "feat")
    return jax.shard_map(shards, mesh=mesh, in_specs=in_specs, out_specs=out_specs, check_vma=False)
```

profile of v0, /device:TPU:2, one launch (start us, length us, event | category | flops | bytes accessed | tf_op | source)
XLA Modules:
  0.0 290.6 jit_solution(7119460857731323404)
XLA Ops:
  10.1 1.6 copy.40
  16.3 73.4 %all-gather.4.cloned.1.call-done = bf16[8192,256]{0,1:T(8,128)(2,1)} async-done(((bf16[128,256]{0,1:T(8,128)(2,1)}), bf16[8192,256]{0,1:T(8,128)(2,1)}) %all-gather.4.cloned.1.call-update) | async-done | bytes 4194320 | tf_op jit(solution)/shard_map/all_gather | solution.py:142
  89.7 78.3 %all-gather.6.cloned.1.call-done = bf16[8192,256]{0,1:T(8,128)(2,1)} async-done(((bf16[128,256]{0,1:T(8,128)(2,1)}), bf16[8192,256]{0,1:T(8,128)(2,1)}) %all-gather.6.cloned.1.call-update) | async-done | bytes 4194320 | tf_op jit(solution)/shard_map/all_gather | solution.py:143
  168.0 75.7 %conditional.1 = (f32[2,4,128]{2,1,0:T(4,128)}, f32[2,4,128,128]{2,3,1,0:T(8,128)S(1)}) conditional(s32[]{:T(128)} %bitcast.3, () %tuple.34, (s32[6]{0:T(128)S(1)}, s32[128]{0:T(128)S(1)}, s32[128]{0:T(128)S(1)}, bf16[8192,256]{0,1:T(8,128)(2,1)}, bf16[128,2,4,128]{3,0,2,1:T(8,128)(2,1)S(1)}, /*index=5*/bf16[8192,256]{0,1:T(8,128)(2,1)}) %tuple.78), branch_computations={%region_3.4_spmd, %region_4.11_spmd} | conditional | flops 275855392 | bytes 10562971 | solution.py:114
  168.2 75.3 %while.19 = (s32[]{:T(128)}, f32[2,4,128]{2,1,0:T(4,128)S(1)}, f32[2,4,128]{2,1,0:T(4,128)}, f32[2,4,128,128]{3,2,1,0:T(8,128)S(1)}, s32[128]{0:T(128)S(1)}, /*i...) while((s32[]{:T(128)}, f32[2,4,128]{2,1,0:T(4,128)S(1)}, ...), condition=%wide.region_10.10_spmd.clone, body=%wide.region_6.9_spmd.clone.sunk | while | flops 275855360 | bytes 9514207 | solution.py:112
  174.7 1.3 fusion.35
  179.5 1.3 fusion.35
  184.2 1.3 fusion.35
  189.0 1.3 fusion.35
  193.7 1.3 fusion.35
  198.5 1.3 fusion.35
  203.2 1.3 fusion.35
  208.0 1.3 fusion.35
  212.7 1.3 fusion.35
  217.4 1.3 fusion.35
  222.2 1.3 fusion.35
  227.0 1.3 fusion.35
  231.7 1.3 fusion.35
  234.0 1.2 constant_dynamic-slice_fusion.3
  236.6 1.3 fusion.35
  241.3 1.3 fusion.35
  244.5 7.3 %all-gather.8.cloned.1.call-done = bf16[1024,4096]{0,1:T(8,128)(2,1)} async-done(((bf16[1024,64]{0,1:T(8,128)(2,1)}), bf16[1024,4096]{0,1:T(8,128)(2,1)}) %all-gather.8.cloned.1.call-update) | async-done | bytes 8388624 | tf_op jit(solution)/shard_map/all_gather | solution.py:151
  251.8 7.3 %convolution_convert_fusion = bf16[128,4096]{1,0:T(8,128)(2,1)} fusion(bf16[128,1024]{0,1:T(8,128)(2,1)S(1)} %bitcast.64, bf16[1024,4096]{0,1:T(8,128)(2,1)} %all-gather.8.cloned.1.call-done), kind=kOutput, calls=%fused_computation.23 | convolution fusion | flops 1074266112 | bytes 9699328 | tf_op jit(solution)/shard_map/dot_general | solution.py:149
  259.1 24.9 %reduce-scatter.2.cloned.1.call-done = bf16[128,1024]{1,0:T(8,128)(2,1)} async-done(((bf16[128,4096]{1,0:T(8,128)(2,1)}), bf16[128,1024]{1,0:T(8,128)(2,1)}) %reduce-scatter.2.cloned.1.call-update) | async-done | bytes 262160 | tf_op jit(solution)/shard_map/reduce_scatter | solution.py:154
  (179 shorter events, 61.6 us)
Async XLA Ops:
  6.5 83.2 %all-gather.4.cloned.1.call-start = ((), (), s32[]{:S(2)}) async-start(), calls=%async_computation.1 | async-start | bytes 4259840 | tf_op jit(solution)/shard_map/all_gather | solution.py:142
  10.1 158.0 %all-gather.6.cloned.1.call-start = ((), (), s32[]{:S(2)}) async-start(), calls=%async_computation.2 | async-start | bytes 4259840 | tf_op jit(solution)/shard_map/all_gather | solution.py:143
  11.7 240.1 %all-gather.8.cloned.1.call-start = ((), (), s32[]{:S(2)}) async-start(), calls=%async_computation.3 | async-start | bytes 8519680 | tf_op jit(solution)/shard_map/all_gather | solution.py:151
  12.4 271.6 %reduce-scatter.2.cloned.1.call-start = ((), (), s32[]{:S(2)}) async-start(), calls=%async_computation.4 | async-start | bytes 1310720 | tf_op jit(solution)/shard_map/reduce_scatter | solution.py:154
  15.7 152.3 %copy-start = (s32[6]{0:T(128)S(1)}, s32[6]{0:T(128)}, u32[]{:S(2)}) copy-start(s32[6]{0:T(128)} %param.13) | copy-start | bytes 76
Sparse Core Ops, SparseCore 0:
  10.2 79.5 all-gather.3
  92.3 75.6 all-gather.5
  170.8 80.9 all-gather.7
  259.3 24.7 reduce-scatter.1
where the time goes:
time: 292 us; the launch traced here: 291 us
  waiting for transfers between devices  185 us (63%)
  other arithmetic  38.1 us (13%)
  matrix products  31 us (11%)
  local copies, waits for them, and re-layouts  21.2 us (7%)
  between operations  14.5 us (5%)
    all_gather x1, waiting for transfers between devices, shards(): lax.all_gather(values, 'tok', axis=0, tiled=True)  78.3 us
    all_gather x1, waiting for transfers between devices, shards(): lax.all_gather(rotated_k, 'tok', axis=0, tiled=True)  73.4 us
    reduce_scatter x1, waiting for transfers between devices, shards(): lax.psum_scatter(partial_terms.astype(jnp.bfloat16), 'feat', scatter_dime...  24.9 us
    add x16, other arithmetic, one_block(): totals = totals * factor + jnp.sum(weights, axis=-1)  20.1 us
    dynamic_slice x16, local copies, waits for them, and re-layouts, one_block(): lax.dynamic_slice_in_dim(value_piece, first_key, block_rows, 0)  17.3 us
    dot_general x16, matrix products, one_block(): jnp.einsum('gjqk,kgd->gjqd', weights.astype(jnp.bfloat16), value_tile, pr...  15.1 us
    dot_general x16, matrix products, one_block(): jnp.einsum('qgjd,kgd->gjqk', query_block, key_tile, preferred_element_typ...  8.59 us
    reduce_sum x16, other arithmetic, one_block(): totals = totals * factor + jnp.sum(weights, axis=-1)  8.35 us
  transfers between devices with their start and end apart: 4, of which 4 were waited for; matrix products, arithmetic and copies ran while one was open for 27% of the time, Pallas kernels for 0%

commit v1 on v0

--- a/solution.py
+++ b/solution.py
@@ -140,7 +140,9 @@
         initial,
         (
             lax.all_gather(rotated_k, "tok", axis=0, tiled=True),
-            lax.all_gather(values, "tok", axis=0, tiled=True),
+            jnp.concatenate(
+                lax.all_to_all(jnp.stack([values] * lax.axis_size("tok")), "tok", 0, 0), axis=0
+            ),
         ),
         jnp.int32(0),
     )

time: 292 us -> 258 us (0.88)
  waiting for transfers between devices: 185 us -> 132 us
  starting transfers between devices: 0.12 us -> 12.4 us
  local copies, waits for them, and re-layouts: 21.2 us -> 28.2 us
    all_gather x1 -> x0, waiting for transfers between devices: 78.3 us -> none  [shards(): lax.all_gather(values, 'tok', axis=0, tiled=True)]
    all_gather x1, waiting for transfers between devices: 73.4 us -> 102 us  [shards(): lax.all_gather(rotated_k, 'tok', axis=0, tiled=True)]
    all_to_all x0 -> x1, starting transfers between devices: none -> 12.3 us  [shards(): lax.all_to_all(jnp.stack([values] * lax.axis_size('tok')), 'tok', 0, 0)]
    reshape x0 -> x1, local copies, waits for them, and re-layouts: none -> 4.76 us  [shards(): jnp.concatenate(lax.all_to_all(jnp.stack([values] * lax.axis_size('tok'))...]
    all_gather x1, waiting for transfers between devices: 7.27 us -> 2.65 us  [shards(): lax.all_gather(out_weight, 'tok', axis=1, tiled=True)]
    another operation x0 -> x1, local copies, waits for them, and re-layouts: none -> 2.95 us  [shards(): jnp.stack([values] * lax.axis_size('tok'))]
  transfers between devices with their start and end apart: 4 -> 4, of which waited for: 4 -> 4; matrix products, arithmetic and copies ran while one was open for 27% -> 33% of each run, Pallas kernels for 0% -> 0%
where the time goes in v1:
time: 258 us; the launch traced here: 256 us
  waiting for transfers between devices  132 us (51%)
  other arithmetic  37.2 us (14%)
  matrix products  31.1 us (12%)
  local copies, waits for them, and re-layouts  28.2 us (11%)
  between operations  14.5 us (6%)
  starting transfers between devices  12.4 us (5%)
    all_gather x1, waiting for transfers between devices, shards(): lax.all_gather(rotated_k, 'tok', axis=0, tiled=True)  102 us
    reduce_scatter x1, waiting for transfers between devices, shards(): lax.psum_scatter(partial_terms.astype(jnp.bfloat16), 'feat', scatter_dime...  24.9 us
    add x16, other arithmetic, one_block(): totals = totals * factor + jnp.sum(weights, axis=-1)  20.1 us
    dynamic_slice x16, local copies, waits for them, and re-layouts, one_block(): lax.dynamic_slice_in_dim(value_piece, first_key, block_rows, 0)  17.2 us
    dot_general x16, matrix products, one_block(): jnp.einsum('gjqk,kgd->gjqd', weights.astype(jnp.bfloat16), value_tile, pr...  15.1 us
    all_to_all x1, starting transfers between devices, shards(): lax.all_to_all(jnp.stack([values] * lax.axis_size('tok')), 'tok', 0, 0)  12.3 us
    dot_general x16, matrix products, one_block(): jnp.einsum('qgjd,kgd->gjqk', query_block, key_tile, preferred_element_typ...  8.64 us
    reduce_sum x16, other arithmetic, one_block(): totals = totals * factor + jnp.sum(weights, axis=-1)  8.37 us
  transfers between devices with their start and end apart: 4, of which 4 were waited for; matrix products, arithmetic and copies ran while one was open for 33% of the time, Pallas kernels for 0%

profile of v1, /device:TPU:2, one launch (start us, length us, event | category | flops | bytes accessed | tf_op | source)
XLA Modules:
  0.0 256.5 jit_solution(6624826881953051217)
XLA Ops:
  11.8 3.0 %stack.2 = bf16[64,128,256]{1,2,0:T(8,128)(2,1)} broadcast(bf16[128,256]{0,1:T(8,128)(2,1)S(1)} %copy.47), dimensions={1,2} | broadcast | bytes 4259840 | tf_op jit(solution)/shard_map/stack | solution.py:144
  14.7 12.3 %all-to-all-start = ((bf16[64,128,256]{1,2,0:T(8,128)(2,1)}), bf16[64,128,256]{1,2,0:T(8,128)(2,1)}, u32[]{:S(2)}, u32[]{:S(2)}) async-start(bf16[64,128,256]{1,2,0:T(8,128)(2,1)} %stack.2), calls=%async_computation | async-start | bytes 8388608 | tf_op jit(solution)/shard_map/all_to_all | solution.py:144
  29.9 101.7 %all-gather.3.cloned.1.call-done = bf16[8192,256]{0,1:T(8,128)(2,1)} async-done(((bf16[128,256]{0,1:T(8,128)(2,1)}), bf16[8192,256]{0,1:T(8,128)(2,1)}) %all-gather.3.cloned.1.call-update) | async-done | bytes 4194320 | tf_op jit(solution)/shard_map/all_gather | solution.py:142
  131.6 2.1 all-to-all-done
  133.7 80.5 %conditional.1 = (f32[2,4,128]{2,1,0:T(4,128)}, f32[2,4,128,128]{2,3,1,0:T(8,128)S(1)}) conditional(s32[]{:T(128)} %bitcast.3, () %tuple.34, (bf16[64,128,256]{1,2,0:T(8,128)(2,1)}, s32[6]{0:T(128)S(1)}, s32[128]{0:T(128)S(1)}, s32[128]{0:T(128)S(1)}, bf16[8192,256]{0,1:T(8,128)(2,1)}, /*index=5*/bf16[128,2,4,128]{3,0,2,1:T(8,128)(2,1)S(1)}) %tuple.79), branch_computations={%region_3.4_spmd, %region_4.11_spmd} | conditional | flops 275855392 | bytes 18951580 | solution.py:114
  133.7 4.8 %copy_bitcast_fusion = bf16[8192,256]{0,1:T(8,128)(2,1)} fusion(bf16[64,128,256]{1,2,0:T(8,128)(2,1)} %get-tuple-element.307), kind=kLoop, calls=%fused_computation.23 | loop fusion | bytes 8388608 | tf_op jit(solution)/shard_map/reshape | solution.py:143
  138.7 75.4 %while.19 = (s32[]{:T(128)}, f32[2,4,128]{2,1,0:T(4,128)S(1)}, f32[2,4,128]{2,1,0:T(4,128)}, f32[2,4,128,128]{3,2,1,0:T(8,128)S(1)}, s32[128]{0:T(128)S(1)}, /*i...) while((s32[]{:T(128)}, f32[2,4,128]{2,1,0:T(4,128)S(1)}, ...), condition=%wide.region_10.10_spmd.clone, body=%wide.region_6.9_spmd.clone.sunk | while | flops 275855360 | bytes 9514207 | solution.py:112
  145.2 1.3 fusion.36
  150.0 1.3 fusion.36
  154.7 1.3 fusion.36
  159.5 1.3 fusion.36
  164.2 1.3 fusion.36
  169.0 1.3 fusion.36
  173.7 1.3 fusion.36
  178.5 1.3 fusion.36
  183.2 1.3 fusion.36
  188.0 1.3 fusion.36
  192.8 1.3 fusion.36
  202.3 1.3 fusion.36
  207.0 1.3 fusion.36
  211.8 1.3 fusion.36
  215.0 2.6 %all-gather.5.cloned.1.call-done = bf16[1024,4096]{0,1:T(8,128)(2,1)} async-done(((bf16[1024,64]{0,1:T(8,128)(2,1)}), bf16[1024,4096]{0,1:T(8,128)(2,1)}) %all-gather.5.cloned.1.call-update) | async-done | bytes 8388624 | tf_op jit(solution)/shard_map/all_gather | solution.py:153
  217.7 7.3 %convolution_convert_fusion = bf16[128,4096]{1,0:T(8,128)(2,1)} fusion(bf16[128,1024]{0,1:T(8,128)(2,1)S(1)} %bitcast.69, bf16[1024,4096]{0,1:T(8,128)(2,1)} %all-gather.5.cloned.1.call-done), kind=kOutput, calls=%fused_computation.24 | convolution fusion | flops 1074266112 | bytes 9699328 | tf_op jit(solution)/shard_map/dot_general | solution.py:151
  225.0 24.9 %reduce-scatter.2.cloned.1.call-done = bf16[128,1024]{1,0:T(8,128)(2,1)} async-done(((bf16[128,4096]{1,0:T(8,128)(2,1)}), bf16[128,1024]{1,0:T(8,128)(2,1)}) %reduce-scatter.2.cloned.1.call-update) | async-done | bytes 262160 | tf_op jit(solution)/shard_map/reduce_scatter | solution.py:156
  (182 shorter events, 63.9 us)
Async XLA Ops:
  6.5 125.1 %all-gather.3.cloned.1.call-start = ((), (), s32[]{:S(2)}) async-start(), calls=%async_computation.2 | async-start | bytes 4259840 | tf_op jit(solution)/shard_map/all_gather | solution.py:142
  10.1 207.6 %all-gather.5.cloned.1.call-start = ((), (), s32[]{:S(2)}) async-start(), calls=%async_computation.3 | async-start | bytes 8519680 | tf_op jit(solution)/shard_map/all_gather | solution.py:153
  14.7 12.6 %copy-start = (bf16[128,1024]{1,0:T(8,128)(2,1)S(1)}, bf16[128,1024]{1,0:T(8,128)(2,1)}, u32[]{:S(2)}) copy-start(bf16[128,1024]{1,0:T(8,128)(2,1)} %param.9) | copy-start | bytes 786436
  14.7 119.0 %all-to-all-start = ((bf16[64,128,256]{1,2,0:T(8,128)(2,1)}), bf16[64,128,256]{1,2,0:T(8,128)(2,1)}, u32[]{:S(2)}, u32[]{:S(2)}) async-start(bf16[64,128,256]{1,2,0:T(8,128)(2,1)} %stack.2), calls=%async_computation | async-start | bytes 8388608 | tf_op jit(solution)/shard_map/all_to_all | solution.py:144
  27.1 222.9 %reduce-scatter.2.cloned.1.call-start = ((), (), s32[]{:S(2)}) async-start(), calls=%async_computation.4 | async-start | bytes 1310720 | tf_op jit(solution)/shard_map/reduce_scatter | solution.py:156
  29.3 104.4 %copy-start.1 = (s32[6]{0:T(128)S(1)}, s32[6]{0:T(128)}, u32[]{:S(2)}) copy-start(s32[6]{0:T(128)} %param.13) | copy-start | bytes 76
Sparse Core Ops, SparseCore 0:
  10.2 121.3 all-gather.2
  134.4 83.2 all-gather.4
  225.1 24.7 reduce-scatter.1
